TPU v7x, 512 devices: a whole 4x4x16 slice. The times are simulated.
512 devices in a mesh: dp: 4 (over x), expert: 128 (over z, y, core).
Axes of the slice: x: 4, y: 4, z: 16, core: 2. Of those that a mesh axis runs over, the one named last changes fastest.
Arguments:
- tokens: bfloat16 [65536, 2048], P(('dp', 'expert')), may hold values from -6 to 6
- hidden_grad: bfloat16 [65536, 1, 768], P(('dp', 'expert')), may hold values from -6 to 6
- gate_prob: float32 [65536, 1], P(('dp', 'expert')), may hold values from 0.2 to 1
- slot_choice: int32 [65536, 1], P(('dp', 'expert')), may hold values from 0 to 127; in each aligned block of 128 rows (0 to 127, 128 to 255, ...) at most 2 rows name the same one
- replica_plan: int32 [128], replicated, may hold values from 0 to 63, as said below
- weights: bfloat16 [64, 2, 2048, 768], P(None, None, ('dp', 'expert')), may hold values from -0.125 to 0.125
Outputs:
- input_grad: bfloat16 [65536, 2048], P(('dp', 'expert'))
- expert_grad: bfloat16 [64, 2, 2048, 768], P(None, None, ('dp', 'expert'))
Inputs may be any that keep to these rules, and one draw needn't show every extreme that they name: `slot_choice`: among the tokens of one device no slot is named more than 2 times, and 2 is reached; the picks of one token name different slots. `replica_plan`: every expert is held by at least one slot.
All inputs are finite; a program needn't handle non-finite values.
Results may differ from a plain program's by a relative error of at most 0.007.
Values may be sent and summed in bfloat16 or wider, within the bound.
A program may use at most 64 MiB of HBM per device.

v0:
```python
import jax
import jax.numpy as jnp
from jax import lax
from jax.sharding import PartitionSpec as P


def back_project(grad_gate, grad_up, weight_pair):
    contract_cols = (((1,), (1,)), ((), ()))
    first_term = lax.dot_general(
        grad_gate, weight_pair[0], contract_cols, preferred_element_type=jnp.float32
    )
    return first_term + lax.dot_general(
        grad_up, weight_pair[1], contract_cols, preferred_element_type=jnp.float32
    )


def row_products(inputs, grad_gate, grad_up):
    contract_rows = (((0,), (0,)), ((), ()))
    return jnp.stack(
        [
            lax.dot_general(inputs, grad_gate, contract_rows, preferred_element_type=jnp.float32),
            lax.dot_general(inputs, grad_up, contract_rows, preferred_element_type=jnp.float32),
        ]
    )


def per_device(tokens, hidden_grad, gate_prob, slot_choice, replica_plan, weights):
    expert_count = lax.axis_size("expert")
    group_count = lax.axis_size("dp")
    token_count, pick_count = slot_choice.shape
    row_count = token_count * pick_count
    capacity = max(2, 2 * row_count // expert_count)
    depth_rows = expert_count * capacity
    model_width = tokens.shape[1]
    hidden_width = hidden_grad.shape[2]
    expert_total = weights.shape[0]
    shard_rows = weights.shape[2]
    block_rows = shard_rows * expert_count
    flat_slot = slot_choice.reshape(row_count)
    slot_member = (flat_slot[:, None] == jnp.arange(expert_count, dtype=jnp.int32)[None, :]).astype(
        jnp.int32
    )
    ranking = jnp.sum((jnp.cumsum(slot_member, axis=0) - 1) * slot_member, axis=1)
    position = flat_slot * capacity + ranking
    scatter_table = (jnp.arange(depth_rows, dtype=jnp.int32)[:, None] == position[None, :]).astype(
        jnp.bfloat16
    )
    token_rows = jnp.repeat(tokens, pick_count, axis=0)
    cotangent = (gate_prob[:, :, None] * hidden_grad.astype(jnp.float32)).astype(jnp.bfloat16)
    cotangent = cotangent.reshape(row_count, hidden_width)
    send_inputs = jnp.dot(scatter_table, token_rows, preferred_element_type=jnp.float32).astype(
        jnp.bfloat16
    )
    send_cotangent = jnp.dot(scatter_table, cotangent, preferred_element_type=jnp.float32).astype(
        jnp.bfloat16
    )
    recv_inputs, recv_cotangent = (
        lax.all_to_all(
            send_inputs.reshape(expert_count, capacity, model_width),
            "expert",
            split_axis=0,
            concat_axis=0,
            tiled=True,
        ),
        lax.all_to_all(
            send_cotangent.reshape(expert_count, capacity, hidden_width),
            "expert",
            split_axis=0,
            concat_axis=0,
            tiled=True,
        ),
    )
    recv_inputs = recv_inputs.reshape(depth_rows, model_width)
    recv_cotangent = recv_cotangent.reshape(depth_rows, hidden_width)
    chooser = (replica_plan[:, None] == jnp.arange(expert_total, dtype=jnp.int32)[None, :]).astype(
        jnp.bfloat16
    )
    send_weights = jnp.einsum(
        "se,ekdf->skdf", chooser, weights, preferred_element_type=jnp.float32
    ).astype(jnp.bfloat16)
    own_weights = lax.all_to_all(
        send_weights, "expert", split_axis=0, concat_axis=2, tiled=True
    ).reshape(2, block_rows, hidden_width)
    piece = lax.all_gather(own_weights, "dp", axis=1, tiled=True)
    gate_sum = jnp.dot(recv_inputs, piece[0], preferred_element_type=jnp.float32)
    up_sum = jnp.dot(recv_inputs, piece[1], preferred_element_type=jnp.float32)
    sigma = jax.nn.sigmoid(gate_sum)
    scaled = recv_cotangent.astype(jnp.float32)
    grad_gate = (scaled * up_sum * sigma * (1.0 + gate_sum * (1.0 - sigma))).astype(jnp.bfloat16)
    grad_up = (scaled * gate_sum * sigma).astype(jnp.bfloat16)
    all_gate, all_up = (
        lax.all_gather(grad_gate, "dp", axis=0, tiled=True),
        lax.all_gather(grad_up, "dp", axis=0, tiled=True),
    )
    split_inputs = recv_inputs.reshape(depth_rows, group_count, block_rows)
    all_columns = lax.all_to_all(
        split_inputs, "dp", split_axis=1, concat_axis=0, tiled=True
    ).reshape(group_count * depth_rows, block_rows)
    row_terms = back_project(all_gate, all_up, own_weights).astype(jnp.bfloat16)
    summed = jnp.zeros((2, block_rows, hidden_width), jnp.float32)
    for group_index in range(group_count):
        lower = group_index * depth_rows
        upper = lower + depth_rows
        products = row_products(
            all_columns[lower:upper], all_gate[lower:upper], all_up[lower:upper]
        )
        summed = summed + lax.optimization_barrier(products.astype(jnp.bfloat16)).astype(
            jnp.float32
        )
    pieces = summed.reshape(2, expert_count, shard_rows, hidden_width)
    gathered = lax.all_to_all(
        pieces.astype(jnp.bfloat16), "expert", split_axis=1, concat_axis=1, tiled=True
    ).astype(pieces.dtype)
    membership = (
        jnp.arange(expert_total, dtype=jnp.int32)[:, None] == replica_plan[None, :]
    ).astype(jnp.float32)
    expert_grad = jnp.einsum("es,ksdf->ekdf", membership, gathered, precision=lax.Precision.HIGHEST)
    expert_grad = (expert_grad / group_count).astype(jnp.bfloat16)
    joined = lax.all_to_all(
        row_terms.reshape(group_count, depth_rows, block_rows),
        "dp",
        split_axis=0,
        concat_axis=2,
        tiled=True,
    )
    back_rows = lax.all_to_all(
        joined.reshape(expert_count, capacity, model_width),
        "expert",
        split_axis=0,
        concat_axis=0,
        tiled=True,
    )
    back_rows = back_rows.reshape(depth_rows, model_width)
    token_grads = lax.dot_general(
        scatter_table, back_rows, (((0,), (0,)), ((), ())), preferred_element_type=jnp.float32
    )
    input_grad = jnp.sum(token_grads.reshape(token_count, pick_count, model_width), axis=1).astype(
        jnp.bfloat16
    )
    return (input_grad, expert_grad)


def solution(mesh):
    placed = (
        P(("dp", "expert"), None),
        P(("dp", "expert"), None, None),
        P(("dp", "expert"), None),
        P(("dp", "expert"), None),
        P(),
        P(None, None, ("dp", "expert"), None),
    )
    return jax.shard_map(
        per_device,
        mesh=mesh,
        in_specs=placed,
        out_specs=(P(("dp", "expert"), None), P(None, None, ("dp", "expert"), None)),
        check_vma=False,
    )
```

profile of v0, /device:TPU:33, one launch (start us, length us, event | category | flops | bytes accessed | tf_op | source)
XLA Modules:
  0.0 494.8 jit_solution(11595988162404496423)
XLA Ops:
  7.2 1.1 copy-done
  8.3 1.3 convolution_convert_fusion.2
  9.6 1.2 copy.26
  10.8 96.8 %all_to_all.65 = bf16[128,2,4,768]{3,2,1,0:T(4,128)(2,1)S(1)} all-to-all(bf16[128,2,4,768]{3,2,1,0:T(4,128)(2,1)S(1)} %copy.26), channel_id=1, replica_groups=mesh['dp'=4,'expert'=128] {'expert'}, dimensions={0} | all-to-all | bytes 3145728 | tf_op jit(solution)/shard_map/all_to_all | solution.py:81
  107.6 2.4 copy.27
  110.0 0.6 copy-done.7
  111.4 0.9 reshape.66
  112.3 7.0 %all-to-all-start = ((bf16[128,2,768]{2,1,0:T(2,128)(2,1)}), bf16[128,2,768]{2,1,0:T(2,128)(2,1)S(1)}, u32[]{:S(2)}, u32[]{:S(2)}) async-start(bf16[128,2,768]{2,1,0:T(2,128)(2,1)} %reshape.66), calls=%async_computation | async-start | bytes 786432 | tf_op jit(solution)/shard_map/all_to_all | solution.py:65
  119.4 1.5 convolution_convert_fusion
  120.9 1.6 reshape.67
  122.5 25.1 %all-to-all-done = bf16[128,2,768]{2,1,0:T(2,128)(2,1)S(1)} async-done(((bf16[128,2,768]{2,1,0:T(2,128)(2,1)}), bf16[128,2,768]{2,1,0:T(2,128)(2,1)S(1)}, u32[]{:S(2)}, u32[]{:S(2)}) %all-to-all-start) | async-done | bytes 393248 | tf_op jit(solution)/shard_map/all_to_all | solution.py:65
  147.6 6.1 %all-to-all-start.1 = ((bf16[128,2,2048]{2,1,0:T(2,128)(2,1)}), bf16[128,2,2048]{2,1,0:T(2,128)(2,1)S(1)}, u32[]{:S(2)}, u32[]{:S(2)}) async-start(bf16[128,2,2048]{2,1,0:T(2,128)(2,1)} %reshape.67), calls=%async_computation.1 | async-start | bytes 2097152 | tf_op jit(solution)/shard_map/all_to_all | solution.py:58
  153.9 1.0 reshape.73
  154.9 54.4 %all-to-all-done.1 = bf16[128,2,2048]{2,1,0:T(2,128)(2,1)S(1)} async-done(((bf16[128,2,2048]{2,1,0:T(2,128)(2,1)}), bf16[128,2,2048]{2,1,0:T(2,128)(2,1)S(1)}, u32[]{:S(2)}, u32[]{:S(2)}) %all-to-all-start.1) | async-done | bytes 1048608 | tf_op jit(solution)/shard_map/all_to_all | solution.py:58
  209.3 1.3 reshape.68
  210.6 12.7 %fusion.40 = (bf16[1,2048,768]{2,0,1:T(2,128)(2,1)S(1)}, bf16[1,2048,768]{2,0,1:T(2,128)(2,1)S(1)}) fusion(bf16[2,2048,768]{2,0,1:T(2,128)(2,1)} %all-gather.4.cloned.1.call-done), kind=kLoop, calls=%fused_computation.69 | loop fusion | bytes 12582912 | tf_op jit(solution)/shard_map/slice | solution.py:85
  223.3 1.8 multiply_convert_fusion.1
  225.1 1.9 fusion.17
  227.1 0.7 all-gather.8.cloned.1.call-update
  227.8 1.4 fusion.41
  229.2 1.6 squeeze.15
  230.9 21.3 %all-gather.6.cloned.1.call-done = bf16[1024,768]{1,0:T(8,128)(2,1)} async-done(((bf16[256,768]{1,0:T(8,128)(2,1)}), bf16[1024,768]{1,0:T(8,128)(2,1)}) %all-gather.6.cloned.1.call-update) | async-done | bytes 1572880 | tf_op jit(solution)/shard_map/all_gather | solution.py:92
  252.3 3.8 fusion.42
  256.0 33.1 %all-gather.8.cloned.1.call-done = bf16[1024,768]{1,0:T(8,128)(2,1)} async-done(((bf16[256,768]{1,0:T(8,128)(2,1)}), bf16[1024,768]{1,0:T(8,128)(2,1)}) %all-gather.8.cloned.1.call-update) | async-done | bytes 1572880 | tf_op jit(solution)/shard_map/all_gather | solution.py:93
  289.1 4.1 add_convert_fusion.1
  293.2 3.5 all-to-all-start.3
  296.7 1.5 reshape_reshape.3
  298.2 2.4 copy.31
  300.6 10.4 %all-to-all-done.3 = bf16[4,256,512]{2,1,0:T(8,128)(2,1)S(1)} async-done(((bf16[4,256,512]{2,1,0:T(8,128)(2,1)}), bf16[4,256,512]{2,1,0:T(8,128)(2,1)S(1)}, u32[]{:S(2)}, u32[]{:S(2)}) %all-to-all-start.3) | async-done | bytes 1048608 | tf_op jit(solution)/shard_map/all_to_all | solution.py:119
  311.0 3.5 all-to-all-start.5
  314.6 1.8 copy.30
  316.3 2.3 reshape.71
  318.6 9.4 %all-to-all-done.5 = bf16[256,4,512]{2,0,1:T(8,128)(2,1)S(1)} async-done(((bf16[256,4,512]{2,0,1:T(8,128)(2,1)}), bf16[256,4,512]{2,0,1:T(8,128)(2,1)S(1)}, u32[]{:S(2)}, u32[]{:S(2)}) %all-to-all-start.5) | async-done | bytes 1048608 | tf_op jit(solution)/shard_map/all_to_all | solution.py:96
  328.0 18.6 %all-to-all-start.4 = ((bf16[128,2,2048]{2,1,0:T(2,128)(2,1)}), bf16[128,2,2048]{2,1,0:T(2,128)(2,1)S(1)}, u32[]{:S(2)}, u32[]{:S(2)}) async-start(bf16[128,2,2048]{2,1,0:T(2,128)(2,1)} %reshape.71), calls=%async_computation.4 | async-start | bytes 2097152 | tf_op jit(solution)/shard_map/all_to_all | solution.py:126
  346.6 1.4 fusion.12
  348.0 1.4 fusion.13
  349.6 1.2 copy-done.2
  351.9 0.4 fusion.6
  353.9 2.0 add_convert_fusion
  355.8 2.9 convert_element_type.82
  358.7 1.7 copy.32
  360.4 41.8 %all-to-all-done.4 = bf16[128,2,2048]{2,1,0:T(2,128)(2,1)S(1)} async-done(((bf16[128,2,2048]{2,1,0:T(2,128)(2,1)}), bf16[128,2,2048]{2,1,0:T(2,128)(2,1)S(1)}, u32[]{:S(2)}, u32[]{:S(2)}) %all-to-all-start.4) | async-done | bytes 1048608 | tf_op jit(solution)/shard_map/all_to_all | solution.py:126
  402.2 6.5 %all-to-all-start.6 = ((bf16[2,128,4,768]{3,2,0,1:T(4,128)(2,1)}), bf16[2,128,4,768]{3,2,0,1:T(4,128)(2,1)S(1)}, u32[]{:S(2)}, u32[]{:S(2)}) async-start(bf16[2,128,4,768]{3,2,0,1:T(4,128)(2,1)} %copy.32), calls=%async_computation.6 | async-start | bytes 3145728 | tf_op jit(solution)/shard_map/all_to_all | solution.py:111
  408.7 1.2 reshape.72
  410.0 2.4 convolution_convert_fusion.1
  412.4 73.8 %all-to-all-done.6 = bf16[2,128,4,768]{3,2,0,1:T(4,128)(2,1)S(1)} async-done(((bf16[2,128,4,768]{3,2,0,1:T(4,128)(2,1)}), bf16[2,128,4,768]{3,2,0,1:T(4,128)(2,1)S(1)}, u32[]{:S(2)}, u32[]{:S(2)}) %all-to-all-start.6) | async-done | bytes 1572896 | tf_op jit(solution)/shard_map/all_to_all | solution.py:111
  486.2 0.5 multiply_convert_fusion
  486.8 1.5 copy.34
  (38 shorter events, 4.0 us)
Async XLA Ops:
  7.2 1.1 copy-start
  7.2 203.4 %all-gather.4.cloned.1.call-start = ((), (), s32[]{:S(2)}) async-start(), calls=%async_computation.7 | async-start | bytes 7864320 | tf_op jit(solution)/shard_map/all_gather | solution.py:84
  110.0 0.7 copy-start.7
  110.0 1.1 copy-start.6
  110.0 1.1 copy-start.9
  112.3 35.2 %all-to-all-start = ((bf16[128,2,768]{2,1,0:T(2,128)(2,1)}), bf16[128,2,768]{2,1,0:T(2,128)(2,1)S(1)}, u32[]{:S(2)}, u32[]{:S(2)}) async-start(bf16[128,2,768]{2,1,0:T(2,128)(2,1)} %reshape.66), calls=%async_computation | async-start | bytes 786432 | tf_op jit(solution)/shard_map/all_to_all | solution.py:65
  147.6 61.7 %all-to-all-start.1 = ((bf16[128,2,2048]{2,1,0:T(2,128)(2,1)}), bf16[128,2,2048]{2,1,0:T(2,128)(2,1)S(1)}, u32[]{:S(2)}, u32[]{:S(2)}) async-start(bf16[128,2,2048]{2,1,0:T(2,128)(2,1)} %reshape.67), calls=%async_computation.1 | async-start | bytes 2097152 | tf_op jit(solution)/shard_map/all_to_all | solution.py:58
  153.7 98.6 %all-gather.6.cloned.1.call-start = ((), (), s32[]{:S(2)}) async-start(), calls=%async_computation.8 | async-start | bytes 1966080 | tf_op jit(solution)/shard_map/all_gather | solution.py:92
  210.6 12.7 %copy-start.5 = (f32[256,768]{1,0:T(8,128)S(1)}, f32[256,768]{1,0:T(8,128)}, u32[]{:S(2)}) copy-start(f32[256,768]{1,0:T(8,128)} %reshape.73) | copy-start | bytes 2359300
  210.6 12.7 %copy-start.4 = (bf16[256,2048]{1,0:T(8,128)(2,1)S(1)}, bf16[256,2048]{1,0:T(8,128)(2,1)}, u32[]{:S(2)}) copy-start(bf16[256,2048]{1,0:T(8,128)(2,1)} %reshape.68) | copy-start | bytes 3145732
  227.0 62.1 %all-gather.8.cloned.1.call-start = ((), (), s32[]{:S(2)}) async-start(), calls=%async_computation.9 | async-start | bytes 1966080 | tf_op jit(solution)/shard_map/all_gather | solution.py:93
  293.2 17.8 %all-to-all-start.3 = ((bf16[4,256,512]{2,1,0:T(8,128)(2,1)}), bf16[4,256,512]{2,1,0:T(8,128)(2,1)S(1)}, u32[]{:S(2)}, u32[]{:S(2)}) async-start(bf16[4,256,512]{2,1,0:T(8,128)(2,1)} %bitcast.99), calls=%async_computation.3 | async-start | bytes 2097152 | tf_op jit(solution)/shard_map/all_to_all | solution.py:119
  311.0 17.0 %all-to-all-start.5 = ((bf16[256,4,512]{2,0,1:T(8,128)(2,1)}), bf16[256,4,512]{2,0,1:T(8,128)(2,1)S(1)}, u32[]{:S(2)}, u32[]{:S(2)}) async-start(bf16[256,4,512]{2,0,1:T(8,128)(2,1)} %copy.31), calls=%async_computation.5 | async-start | bytes 2097152 | tf_op jit(solution)/shard_map/all_to_all | solution.py:96
  328.0 74.2 %all-to-all-start.4 = ((bf16[128,2,2048]{2,1,0:T(2,128)(2,1)}), bf16[128,2,2048]{2,1,0:T(2,128)(2,1)S(1)}, u32[]{:S(2)}, u32[]{:S(2)}) async-start(bf16[128,2,2048]{2,1,0:T(2,128)(2,1)} %reshape.71), calls=%async_computation.4 | async-start | bytes 2097152 | tf_op jit(solution)/shard_map/all_to_all | solution.py:126
  349.5 1.4 copy-start.2
  349.5 1.9 copy-start.3
  402.2 84.0 %all-to-all-start.6 = ((bf16[2,128,4,768]{3,2,0,1:T(4,128)(2,1)}), bf16[2,128,4,768]{3,2,0,1:T(4,128)(2,1)S(1)}, u32[]{:S(2)}, u32[]{:S(2)}) async-start(bf16[2,128,4,768]{3,2,0,1:T(4,128)(2,1)} %copy.32), calls=%async_computation.6 | async-start | bytes 3145728 | tf_op jit(solution)/shard_map/all_to_all | solution.py:111
  408.7 77.5 %copy-start.8 = (s32[128]{0:T(128)S(1)}, s32[128]{0:T(128)}, u32[]{:S(2)}) copy-start(s32[128]{0:T(128)} %param.10) | copy-start | bytes 1540
  410.0 78.3 %copy-start.1 = (bf16[64,2,4,768]{3,2,1,0:T(4,128)(2,1)S(1)}, bf16[64,2,4,768]{3,2,1,0:T(4,128)(2,1)}, u32[]{:S(2)}) copy-start(bf16[64,2,4,768]{3,2,1,0:T(4,128)(2,1)} %param.11) | copy-start | bytes 2359300
Sparse Core Ops, SparseCore 0:
  110.1 64.8 all-gather.3
  227.1 25.0 all-gather.5
  254.9 34.1 all-gather.7
where the time goes:
time: 496 us; the launch traced here: 495 us
  waiting for transfers between devices  270 us (54%)
  blocking collectives  96.8 us (20%)
  starting transfers between devices  45.6 us (9%)
  local copies, waits for them, and re-layouts  42.5 us (9%)
  matrix products  22.8 us (5%)
  between operations  14 us (3%)
    all_to_all x1, blocking collectives, per_device(): lax.all_to_all(send_weights, 'expert', split_axis=0, concat_axis=2, tiled...  96.8 us
    all_to_all x1, waiting for transfers between devices, per_device(): lax.all_to_all(pieces.astype(jnp.bfloat16), 'expert', split_axis=1, conca...  73.8 us
    all_to_all x1, waiting for transfers between devices, per_device(): lax.all_to_all(send_inputs.reshape(expert_count, capacity, model_width),...  54.4 us
    all_to_all x1, waiting for transfers between devices, per_device(): lax.all_to_all(joined.reshape(expert_count, capacity, model_width), 'expe...  41.8 us
    all_gather x1, waiting for transfers between devices, per_device(): lax.all_gather(grad_up, 'dp', axis=0, tiled=True)  33.1 us
    all_to_all x1, waiting for transfers between devices, per_device(): lax.all_to_all(send_cotangent.reshape(expert_count, capacity, hidden_widt...  25.1 us
    all_gather x1, waiting for transfers between devices, per_device(): lax.all_gather(grad_gate, 'dp', axis=0, tiled=True)  21.3 us
    all_to_all x1, starting transfers between devices, per_device(): lax.all_to_all(joined.reshape(expert_count, capacity, model_width), 'expe...  18.6 us
  transfers between devices with their start and end apart: 9, of which 8 were waited for; matrix products, arithmetic and copies ran while one was open for 8% of the time, Pallas kernels for 0%

commit v1 on v0

--- a/solution.py
+++ b/solution.py
@@ -2,6 +2,28 @@
 import jax.numpy as jnp
 from jax import lax
 from jax.sharding import PartitionSpec as P
+
+
+def joined_along(blocks, dim):
+    dims = list(blocks.shape[1:])
+    dims[dim] *= blocks.shape[0]
+    return jnp.moveaxis(blocks, 0, dim).reshape(dims)
+
+
+def ring_gather(x, axis, dim):
+    length = lax.axis_size(axis)
+    pairs = [(i, (i + 1) % length) for i in range(length)]
+    back = [(b, a) for a, b in pairs]
+    lower, upper = ([], [])
+    for step in range(length - 1):
+        if step % 2 == 0:
+            lower.append(lax.ppermute(lower[-1] if lower else x, axis, pairs))
+        else:
+            upper.append(lax.ppermute(upper[-1] if upper else x, axis, back))
+    blocks = jnp.stack([*lower[::-1], x, *upper])
+    shift = lax.axis_index(axis) - len(lower)
+    blocks = blocks[(jnp.arange(length) - shift) % length]
+    return joined_along(blocks, dim)
 
 
 def back_project(grad_gate, grad_up, weight_pair):
@@ -90,7 +112,7 @@
     grad_up = (scaled * gate_sum * sigma).astype(jnp.bfloat16)
     all_gate, all_up = (
         lax.all_gather(grad_gate, "dp", axis=0, tiled=True),
-        lax.all_gather(grad_up, "dp", axis=0, tiled=True),
+        ring_gather(grad_up, "dp", 0),
     )
     split_inputs = recv_inputs.reshape(depth_rows, group_count, block_rows)
     all_columns = lax.all_to_all(

time: 496 us -> 467 us (0.942)
  waiting for transfers between devices: 270 us -> 239 us
  matrix products: 22.8 us -> 16.3 us
    all_gather x1 -> x0, waiting for transfers between devices: 33.1 us -> none  [per_device(): lax.all_gather(grad_up, 'dp', axis=0, tiled=True)]
    all_gather x1, waiting for transfers between devices: 21.3 us -> 0.01 us  [per_device(): lax.all_gather(grad_gate, 'dp', axis=0, tiled=True)]
    ppermute x0 -> x3, waiting for transfers between devices: none -> 20.6 us  [the longest x2 20.6 us: ring_gather(): lower.append(lax.ppermute(lower[-1] if lower else x, axis, pairs))]
    ppermute x0 -> x3, starting transfers between devices: none -> 9.35 us  [the longest x2 5.98 us: ring_gather(): lower.append(lax.ppermute(lower[-1] if lower else x, axis, pairs))]
    all_to_all x1, starting transfers between devices: 18.6 us -> 13 us  [per_device(): lax.all_to_all(joined.reshape(expert_count, capacity, model_width), 'expe...]
  transfers between devices with their start and end apart: 9 -> 11, of which waited for: 8 -> 8; matrix products, arithmetic and copies ran while one was open for 8% -> 8% of each run, Pallas kernels for 0% -> 0%
where the time goes in v1:
time: 467 us; the launch traced here: 466 us
  waiting for transfers between devices  239 us (51%)
  blocking collectives  96.8 us (21%)
  starting transfers between devices  49.3 us (11%)
  local copies, waits for them, and re-layouts  45.7 us (10%)
  matrix products  16.3 us (3%)
  between operations  14.4 us (3%)
    all_to_all x1, blocking collectives, per_device(): lax.all_to_all(send_weights, 'expert', split_axis=0, concat_axis=2, tiled...  96.8 us
    all_to_all x1, waiting for transfers between devices, per_device(): lax.all_to_all(pieces.astype(jnp.bfloat16), 'expert', split_axis=1, conca...  74.9 us
    all_to_all x1, waiting for transfers between devices, per_device(): lax.all_to_all(send_inputs.reshape(expert_count, capacity, model_width),...  54.4 us
    all_to_all x1, waiting for transfers between devices, per_device(): lax.all_to_all(joined.reshape(expert_count, capacity, model_width), 'expe...  44.1 us
    all_to_all x1, waiting for transfers between devices, per_device(): lax.all_to_all(send_cotangent.reshape(expert_count, capacity, hidden_widt...  25.1 us
    ppermute x2, waiting for transfers between devices, ring_gather(): lower.append(lax.ppermute(lower[-1] if lower else x, axis, pairs))  20.6 us
    all_to_all x1, starting transfers between devices, per_device(): lax.all_to_all(joined.reshape(expert_count, capacity, model_width), 'expe...  13 us
    slice x1, local copies, waits for them, and re-layouts, per_device(): piece[0]  12.7 us
  transfers between devices with their start and end apart: 11, of which 8 were waited for; matrix products, arithmetic and copies ran while one was open for 8% of the time, Pallas kernels for 0%

profile of v1, /device:TPU:33, one launch (start us, length us, event | category | flops | bytes accessed | tf_op | source)
XLA Modules:
  0.0 465.9 jit_solution(16628256253140691697)
XLA Ops:
  7.2 1.1 copy-done
  8.3 1.3 convolution_convert_fusion.2
  9.6 1.2 copy.26
  10.8 96.8 %all_to_all.65 = bf16[128,2,4,768]{3,2,1,0:T(4,128)(2,1)S(1)} all-to-all(bf16[128,2,4,768]{3,2,1,0:T(4,128)(2,1)S(1)} %copy.26), channel_id=1, replica_groups=mesh['dp'=4,'expert'=128] {'expert'}, dimensions={0} | all-to-all | bytes 3145728 | tf_op jit(solution)/shard_map/all_to_all | solution.py:103
  107.6 2.4 copy.27
  111.4 0.9 reshape.122
  112.3 7.0 %all-to-all-start = ((bf16[128,2,768]{2,1,0:T(2,128)(2,1)}), bf16[128,2,768]{2,1,0:T(2,128)(2,1)S(1)}, u32[]{:S(2)}, u32[]{:S(2)}) async-start(bf16[128,2,768]{2,1,0:T(2,128)(2,1)} %reshape.122), calls=%async_computation | async-start | bytes 786432 | tf_op jit(solution)/shard_map/all_to_all | solution.py:87
  119.4 1.5 convolution_convert_fusion
  120.9 1.6 reshape.123
  122.5 25.1 %all-to-all-done = bf16[128,2,768]{2,1,0:T(2,128)(2,1)S(1)} async-done(((bf16[128,2,768]{2,1,0:T(2,128)(2,1)}), bf16[128,2,768]{2,1,0:T(2,128)(2,1)S(1)}, u32[]{:S(2)}, u32[]{:S(2)}) %all-to-all-start) | async-done | bytes 393248 | tf_op jit(solution)/shard_map/all_to_all | solution.py:87
  147.5 6.1 %all-to-all-start.1 = ((bf16[128,2,2048]{2,1,0:T(2,128)(2,1)}), bf16[128,2,2048]{2,1,0:T(2,128)(2,1)S(1)}, u32[]{:S(2)}, u32[]{:S(2)}) async-start(bf16[128,2,2048]{2,1,0:T(2,128)(2,1)} %reshape.123), calls=%async_computation.1 | async-start | bytes 2097152 | tf_op jit(solution)/shard_map/all_to_all | solution.py:80
  153.9 1.0 reshape.130
  154.9 54.4 %all-to-all-done.1 = bf16[128,2,2048]{2,1,0:T(2,128)(2,1)S(1)} async-done(((bf16[128,2,2048]{2,1,0:T(2,128)(2,1)}), bf16[128,2,2048]{2,1,0:T(2,128)(2,1)S(1)}, u32[]{:S(2)}, u32[]{:S(2)}) %all-to-all-start.1) | async-done | bytes 1048608 | tf_op jit(solution)/shard_map/all_to_all | solution.py:80
  209.3 1.3 reshape.124
  210.5 12.7 %fusion.38 = (bf16[1,2048,768]{2,0,1:T(2,128)(2,1)S(1)}, bf16[1,2048,768]{2,0,1:T(2,128)(2,1)S(1)}) fusion(bf16[2,2048,768]{2,0,1:T(2,128)(2,1)} %all-gather.3.cloned.1.call-done), kind=kLoop, calls=%fused_computation.78 | loop fusion | bytes 12582912 | tf_op jit(solution)/shard_map/slice | solution.py:107
  223.3 1.8 multiply_convert_fusion.1
  225.1 1.9 fusion.17
  227.1 3.1 collective-permute-start
  230.2 3.4 collective-permute-start.2
  233.6 8.7 %collective-permute-done = bf16[256,768]{1,0:T(8,128)(2,1)} collective-permute-done((bf16[256,768]{1,0:T(8,128)(2,1)}, bf16[256,768]{1,0:T(8,128)(2,1)}, u32[]{:S(2)}, u32[]{:S(2)}) %collective-permute-start) | collective-permute-done | bytes 393248 | tf_op jit(solution)/shard_map/ppermute | solution.py:20
  242.2 2.9 collective-permute-start.1
  245.1 1.4 fusion.39
  246.5 2.3 squeeze.14
  248.8 1.1 squeeze.15
  249.9 12.0 %collective-permute-done.1 = bf16[256,768]{1,0:T(8,128)(2,1)} collective-permute-done((bf16[256,768]{1,0:T(8,128)(2,1)}, bf16[256,768]{1,0:T(8,128)(2,1)}, u32[]{:S(2)}, u32[]{:S(2)}) %collective-permute-start.1) | collective-permute-done | bytes 393248 | tf_op jit(solution)/shard_map/ppermute | solution.py:20
  261.8 1.5 pad_maximum_fusion
  263.4 1.8 gather_fusion
  265.2 2.6 fusion.40
  267.8 2.0 add_convert_fusion.1
  269.8 3.5 all-to-all-start.3
  273.3 1.5 reshape_reshape.3
  274.8 2.4 copy.31
  277.2 10.0 %all-to-all-done.3 = bf16[4,256,512]{2,1,0:T(8,128)(2,1)S(1)} async-done(((bf16[4,256,512]{2,1,0:T(8,128)(2,1)}), bf16[4,256,512]{2,1,0:T(8,128)(2,1)S(1)}, u32[]{:S(2)}, u32[]{:S(2)}) %all-to-all-start.3) | async-done | bytes 1048608 | tf_op jit(solution)/shard_map/all_to_all | solution.py:141
  287.2 1.0 copy-done.4
  288.2 3.5 all-to-all-start.5
  291.7 2.0 copy.30
  293.8 1.2 reshape.128
  295.0 9.8 %all-to-all-done.5 = bf16[256,4,512]{2,0,1:T(8,128)(2,1)S(1)} async-done(((bf16[256,4,512]{2,0,1:T(8,128)(2,1)}), bf16[256,4,512]{2,0,1:T(8,128)(2,1)S(1)}, u32[]{:S(2)}, u32[]{:S(2)}) %all-to-all-start.5) | async-done | bytes 1048608 | tf_op jit(solution)/shard_map/all_to_all | solution.py:118
  304.8 13.0 %all-to-all-start.4 = ((bf16[128,2,2048]{2,1,0:T(2,128)(2,1)}), bf16[128,2,2048]{2,1,0:T(2,128)(2,1)}, u32[]{:S(2)}, u32[]{:S(2)}) async-start(bf16[128,2,2048]{2,1,0:T(2,128)(2,1)} %reshape.128), calls=%async_computation.4 | async-start | bytes 2097152 | tf_op jit(solution)/shard_map/all_to_all | solution.py:148
  322.3 2.0 add_convert_fusion
  324.2 2.9 convert_element_type.82
  327.1 1.7 copy.32
  328.9 44.1 %all-to-all-done.4 = bf16[128,2,2048]{2,1,0:T(2,128)(2,1)} async-done(((bf16[128,2,2048]{2,1,0:T(2,128)(2,1)}), bf16[128,2,2048]{2,1,0:T(2,128)(2,1)}, u32[]{:S(2)}, u32[]{:S(2)}) %all-to-all-start.4) | async-done | bytes 1048608 | tf_op jit(solution)/shard_map/all_to_all | solution.py:148
  373.0 6.5 %all-to-all-start.6 = ((bf16[2,128,4,768]{3,2,0,1:T(4,128)(2,1)}), bf16[2,128,4,768]{3,2,0,1:T(4,128)(2,1)S(1)}, u32[]{:S(2)}, u32[]{:S(2)}) async-start(bf16[2,128,4,768]{3,2,0,1:T(4,128)(2,1)} %copy.32), calls=%async_computation.6 | async-start | bytes 3145728 | tf_op jit(solution)/shard_map/all_to_all | solution.py:133
  379.5 1.5 reshape.129
  381.0 1.1 convolution_convert_fusion.1
  382.1 74.9 %all-to-all-done.6 = bf16[2,128,4,768]{3,2,0,1:T(4,128)(2,1)S(1)} async-done(((bf16[2,128,4,768]{3,2,0,1:T(4,128)(2,1)}), bf16[2,128,4,768]{3,2,0,1:T(4,128)(2,1)S(1)}, u32[]{:S(2)}, u32[]{:S(2)}) %all-to-all-start.6) | async-done | bytes 1572896 | tf_op jit(solution)/shard_map/all_to_all | solution.py:133
  457.5 1.5 copy.34
  (53 shorter events, 6.7 us)
Async XLA Ops:
  7.2 1.1 copy-start
  7.2 203.4 %all-gather.3.cloned.1.call-start = ((), (), s32[]{:S(2)}) async-start(), calls=%async_computation.7 | async-start | bytes 7864320 | tf_op jit(solution)/shard_map/all_gather | solution.py:106
  110.0 0.7 copy-start.11
  110.0 1.1 copy-start.10
  110.0 1.1 copy-start.13
  112.3 35.2 %all-to-all-start = ((bf16[128,2,768]{2,1,0:T(2,128)(2,1)}), bf16[128,2,768]{2,1,0:T(2,128)(2,1)S(1)}, u32[]{:S(2)}, u32[]{:S(2)}) async-start(bf16[128,2,768]{2,1,0:T(2,128)(2,1)} %reshape.122), calls=%async_computation | async-start | bytes 786432 | tf_op jit(solution)/shard_map/all_to_all | solution.py:87
  147.5 61.7 %all-to-all-start.1 = ((bf16[128,2,2048]{2,1,0:T(2,128)(2,1)}), bf16[128,2,2048]{2,1,0:T(2,128)(2,1)S(1)}, u32[]{:S(2)}, u32[]{:S(2)}) async-start(bf16[128,2,2048]{2,1,0:T(2,128)(2,1)} %reshape.123), calls=%async_computation.1 | async-start | bytes 2097152 | tf_op jit(solution)/shard_map/all_to_all | solution.py:80
  153.7 111.5 %all-gather.5.cloned.1.call-start = ((), (), s32[]{:S(2)}) async-start(), calls=%async_computation.8 | async-start | bytes 1966080 | tf_op jit(solution)/shard_map/all_gather | solution.py:114
  210.5 12.8 %copy-start.9 = (f32[256,768]{1,0:T(8,128)S(1)}, f32[256,768]{1,0:T(8,128)}, u32[]{:S(2)}) copy-start(f32[256,768]{1,0:T(8,128)} %reshape.130) | copy-start | bytes 2359300
  210.5 12.8 %copy-start.6 = (bf16[256,2048]{1,0:T(8,128)(2,1)S(1)}, bf16[256,2048]{1,0:T(8,128)(2,1)}, u32[]{:S(2)}) copy-start(bf16[256,2048]{1,0:T(8,128)(2,1)} %reshape.124) | copy-start | bytes 3145732
  227.1 15.2 %collective-permute-start = (bf16[256,768]{1,0:T(8,128)(2,1)}, bf16[256,768]{1,0:T(8,128)(2,1)}, u32[]{:S(2)}, u32[]{:S(2)}) collective-permute-start(bf16[256,768]{1,0:T(8,128)(2,1)} %get-tuple-element.14), channel_id=1, source_target_pairs={{0,128},{128,256},{256,384},{384,0},{1,129},{129,257},{257,385},{3... | collective-permute-start | bytes 1179656 | tf_op jit(solution)/shard_map/ppermute | solution.py:20
  230.2 19.7 %collective-permute-start.2 = (bf16[256,768]{1,0:T(8,128)(2,1)}, bf16[256,768]{1,0:T(8,128)(2,1)}, u32[]{:S(2)}, u32[]{:S(2)}) collective-permute-start(bf16[256,768]{1,0:T(8,128)(2,1)} %get-tuple-element.14), channel_id=1, source_target_pairs={{128,0},{256,128},{384,256},{0,384},{129,1},{257,129},{385,257},{1... | collective-permute-start | bytes 1179656 | tf_op jit(solution)/shard_map/ppermute | solution.py:22
  242.2 19.6 %collective-permute-start.1 = (bf16[256,768]{1,0:T(8,128)(2,1)}, bf16[256,768]{1,0:T(8,128)(2,1)}, u32[]{:S(2)}, u32[]{:S(2)}) collective-permute-start(bf16[256,768]{1,0:T(8,128)(2,1)} %collective-permute-done), channel_id=1, source_target_pairs={{0,128},{128,256},{256,384},{384,0},{1,129},{129,257},{257,385},{3... | collective-permute-start | bytes 1179656 | tf_op jit(solution)/shard_map/ppermute | solution.py:20
  263.4 1.8 copy-start.7
  265.2 2.6 copy-start.2
  265.2 2.6 copy-start.8
  269.8 17.4 %all-to-all-start.3 = ((bf16[4,256,512]{2,1,0:T(8,128)(2,1)}), bf16[4,256,512]{2,1,0:T(8,128)(2,1)S(1)}, u32[]{:S(2)}, u32[]{:S(2)}) async-start(bf16[4,256,512]{2,1,0:T(8,128)(2,1)} %bitcast.119), calls=%async_computation.3 | async-start | bytes 2097152 | tf_op jit(solution)/shard_map/all_to_all | solution.py:141
  287.2 1.0 copy-start.4
  288.2 16.6 %all-to-all-start.5 = ((bf16[256,4,512]{2,0,1:T(8,128)(2,1)}), bf16[256,4,512]{2,0,1:T(8,128)(2,1)S(1)}, u32[]{:S(2)}, u32[]{:S(2)}) async-start(bf16[256,4,512]{2,0,1:T(8,128)(2,1)} %copy.31), calls=%async_computation.5 | async-start | bytes 2097152 | tf_op jit(solution)/shard_map/all_to_all | solution.py:118
  295.0 22.8 %copy-start.3 = (bf16[4,256,768]{2,1,0:T(8,128)(2,1)S(1)}, bf16[4,256,768]{2,1,0:T(8,128)(2,1)}, u32[]{:S(2)}) copy-start(bf16[4,256,768]{2,1,0:T(8,128)(2,1)} %gather_fusion) | copy-start | bytes 4718596
  304.8 68.2 %all-to-all-start.4 = ((bf16[128,2,2048]{2,1,0:T(2,128)(2,1)}), bf16[128,2,2048]{2,1,0:T(2,128)(2,1)}, u32[]{:S(2)}, u32[]{:S(2)}) async-start(bf16[128,2,2048]{2,1,0:T(2,128)(2,1)} %reshape.128), calls=%async_computation.4 | async-start | bytes 2097152 | tf_op jit(solution)/shard_map/all_to_all | solution.py:148
  318.6 1.4 copy-start.5
  373.0 84.0 %all-to-all-start.6 = ((bf16[2,128,4,768]{3,2,0,1:T(4,128)(2,1)}), bf16[2,128,4,768]{3,2,0,1:T(4,128)(2,1)S(1)}, u32[]{:S(2)}, u32[]{:S(2)}) async-start(bf16[2,128,4,768]{3,2,0,1:T(4,128)(2,1)} %copy.32), calls=%async_computation.6 | async-start | bytes 3145728 | tf_op jit(solution)/shard_map/all_to_all | solution.py:133
  379.5 77.5 %copy-start.12 = (s32[128]{0:T(128)S(1)}, s32[128]{0:T(128)}, u32[]{:S(2)}) copy-start(s32[128]{0:T(128)} %param.10) | copy-start | bytes 1540
  381.0 78.0 %copy-start.1 = (bf16[64,2,4,768]{3,2,1,0:T(4,128)(2,1)S(1)}, bf16[64,2,4,768]{3,2,1,0:T(4,128)(2,1)}, u32[]{:S(2)}) copy-start(bf16[64,2,4,768]{3,2,1,0:T(4,128)(2,1)} %param.11) | copy-start | bytes 2359300
Sparse Core Ops, SparseCore 0:
  110.1 64.8 all-gather.2
  227.2 31.6 all-gather.4
